TPU v7x, 32 devices: a whole 2x2x4 slice. The times are simulated.
32 devices in a mesh: band: 8 (over z, x), coef: 4 (over y, core).
Axes of the slice: x: 2, y: 2, z: 4, core: 2. Of those that a mesh axis runs over, the one named last changes fastest.
Arguments:
- coeffs: float32 [1024, 262144], P('band', 'coef'), may hold values from -320 to 320
- ref_block: float32 [1024, 262144], P('band', 'coef'), may hold values from -0.01171875 to 0.01171875
- index_map: int32 [262144], P('coef'), may hold values from 0 to 65535, as said below
- band_group: int32 [1024], P('band'), may hold values from 0 to 15
Outputs:
- ortho: float32 [1024, 262144], P('band', 'coef')
- band_residual: float32 [1024], P('band')
- group_residual: float32 [16], replicated
Inputs may be any that keep to these rules, and one draw needn't show every extreme that they name: Within each aligned slab of 65536 coefficients, index_map holds every number of 0 to 65535 once.
All inputs are finite; a program needn't handle non-finite values.
Results may differ from a plain program's by a relative error of at most 0.000098.
Values sent between devices are 32-bit elements; how exact they have to be, the bound alone decides.
A program may use at most 384 MiB of HBM per device.

v0:
```python
import jax
import jax.numpy as jnp
from jax import lax
from jax.sharding import PartitionSpec as P

NB = 1024
NGROUPS = 16


def local(coeffs, ref_block, index_map, band_group):
    columns = lax.all_to_all(coeffs, "band", split_axis=1, concat_axis=0, tiled=True)
    partial_value = jnp.dot(
        columns, columns.T, precision=lax.Precision.HIGHEST, preferred_element_type=jnp.float32
    )
    margin = lax.psum(partial_value, ("band", "coef"))
    factor = jnp.linalg.cholesky(margin)
    ortho_cols = lax.linalg.triangular_solve(factor, columns, left_side=True, lower=True)
    ortho = lax.all_to_all(ortho_cols, "band", split_axis=0, concat_axis=1, tiled=True)
    aligned = jnp.take(ortho, index_map, axis=1)
    squares = jnp.sum((aligned - ref_block) ** 2, axis=1)
    group_range = jnp.arange(NGROUPS, dtype=jnp.int32)
    totals = lax.psum(squares, "coef")
    band_residual = jnp.sqrt(totals + 1e-06)
    onehot = (band_group[:, None] == group_range[None, :]).astype(jnp.float32)
    terms = jnp.dot(
        band_residual, onehot, precision=lax.Precision.HIGHEST, preferred_element_type=jnp.float32
    )
    group_residual = lax.psum(terms, "band") * (NGROUPS / NB)
    return (ortho, band_residual, group_residual)


def solution(mesh):
    return jax.shard_map(
        local,
        mesh=mesh,
        in_specs=(P("band", "coef"), P("band", "coef"), P("coef"), P("band")),
        out_specs=(P("band", "coef"), P("band"), P()),
        check_vma=False,
    )
```

profile of v0, /device:TPU:0, one launch (start us, length us, event | category | flops | bytes accessed | tf_op | source)
XLA Modules:
  0.0 2639.6 jit_solution(11342121475017291769)
XLA Ops:
  7.2 33.4 %copy.17 = f32[128,65536]{0,1:T(8,128)} copy(f32[128,65536]{1,0:T(8,128)} %param.4) | data formatting | bytes 67108864 | tf_op args[0]
  40.6 31.1 %copy.18 = f32[128,8,8192]{2,0,1:T(8,128)} copy(f32[128,8,8192]{0,2,1:T(8,128)} %bitcast.156) | data formatting | bytes 67108864 | tf_op jit(solution)/shard_map/all_to_all | solution.py:11
  71.7 735.1 %all_to_all.38 = f32[128,8,8192]{2,0,1:T(8,128)} all-to-all(f32[128,8,8192]{2,0,1:T(8,128)} %copy.18), channel_id=1, replica_groups=mesh['band'=8,'coef'=4] {'band'}, dimensions={1} | all-to-all | bytes 67108864 | tf_op jit(solution)/shard_map/all_to_all | solution.py:11
  806.8 117.0 %fusion.74 = f32[1024,1024]{0,1:T(8,128)} fusion(f32[1024,8192]{1,0:T(8,128)} %bitcast.157), kind=kOutput, calls=%fused_computation.177 | convolution fusion | flops 103079215104 | bytes 37748736 | tf_op jit(solution)/shard_map/dot_general | solution.py:12
  923.9 141.9 %all-reduce.3.cloned.1.call-done = f32[1024,1024]{0,1:T(8,128)} async-done(((f32[1024,1024]{0,1:T(8,128)}), f32[1024,1024]{0,1:T(8,128)}) %all-reduce.3.cloned.1.call-update) | async-done | bytes 4194320 | tf_op jit(solution)/shard_map/psum | solution.py:15
  1065.7 5.5 copy.20
  1077.7 11.7 cholesky.223
  1089.5 9.8 custom-call.62
  1105.7 11.9 cholesky.244
  1118.2 9.8 custom-call.63
  1131.4 11.7 cholesky.468
  1144.4 9.8 custom-call.64
  1157.7 12.1 cholesky.487
  1171.0 9.8 custom-call.65
  1184.3 11.7 cholesky.506
  1197.3 10.0 custom-call.66
  1210.6 11.7 cholesky.526
  1223.6 9.8 custom-call.67
  1236.4 11.9 cholesky.546
  1249.6 9.8 custom-call.68
  1262.1 11.7 cholesky.564
  1280.8 4.8 select_select_fusion
  1285.6 23.2 while.1
  1308.8 79.0 %custom-call.69 = f32[8,128,128]{1,2,0:T(8,128)S(1)} custom-call(f32[8,128,128]{2,1,0:T(8,128)S(1)} %get-tuple-element.10), custom_call_target="InvertDiagBlocksLowerTriangular" | custom-call | tf_op jit(solution)/shard_map/triangular_solve | solution.py:17
  1387.8 12.6 constant_dynamic-update-slice_fusion.17
  1400.4 6.9 convolution_subtract_fusion.1
  1407.3 8.2 constant_dynamic-update-slice_fusion.16
  1415.5 7.7 convolution_subtract_fusion
  1423.2 8.4 constant_dynamic-update-slice_fusion.15
  1431.6 12.2 fusion.16
  1443.8 13.9 constant_dynamic-update-slice_fusion.14
  1457.7 14.1 fusion.19
  1471.8 12.5 constant_dynamic-update-slice_fusion.13
  1484.3 17.1 convolution_subtract_fusion.2
  1501.4 6.7 constant_dynamic-update-slice_fusion.12
  1508.2 19.3 convolution_subtract_fusion.4
  1527.5 5.8 constant_dynamic-update-slice_fusion.11
  1533.3 23.5 convolution_subtract_fusion.3
  1556.8 7.9 convolution_dynamic-update-slice_fusion
  1564.7 7.1 all-to-all-start.1
  1571.8 33.4 %copy.22 = f32[128,65536]{0,1:T(8,128)} copy(f32[128,65536]{1,0:T(8,128)} %param.5) | data formatting | bytes 67108864 | tf_op args[1]
  1605.4 687.3 %all-to-all-done.1 = f32[8,128,8192]{2,1,0:T(8,128)} async-done(((f32[8,128,8192]{2,1,0:T(8,128)}), f32[8,128,8192]{2,1,0:T(8,128)}, u32[]{:S(2)}, u32[]{:S(2)}) %all-to-all-start.1) | async-done | bytes 33554464 | tf_op jit(solution)/shard_map/all_to_all | solution.py:18
  2292.7 31.0 %copy.21 = f32[128,8,8192]{0,2,1:T(8,128)} copy(f32[128,8,8192]{2,0,1:T(8,128)} %bitcast.35) | data formatting | bytes 67108864 | tf_op jit(solution)/shard_map/all_to_all | solution.py:18
  2323.7 228.0 %gather_fusion = f32[65536,128]{1,0:T(8,128)} fusion(f32[128,65536]{0,1:T(8,128)} %bitcast.154, s32[65536]{0:T(1024)S(1)} %fusion.45), kind=kCustom, calls=%fused_computation | custom fusion | bytes 67371008 | tf_op jit(solution)/shard_map/jit(_take)/gather | solution.py:19
  2551.7 20.7 fusion.1
  2572.4 5.7 psum.22
  2578.3 33.5 %copy.23 = f32[128,65536]{1,0:T(8,128)} copy(f32[128,65536]{0,1:T(8,128)} %bitcast.155) | data formatting | bytes 67108864
  2611.7 20.3 psum.23
  (86 shorter events, 65.2 us)
Async XLA Ops:
  7.2 1058.6 %all-reduce.3.cloned.1.call-start = ((), (), s32[]{:S(2)}) async-start(), calls=%async_computation.2 | async-start | bytes 8388608 | tf_op jit(solution)/shard_map/psum | solution.py:15
  1075.7 2.0 copy-start.3
  1400.4 31.3 %copy-start = (f32[128,8192]{1,0:T(8,128)}, f32[128,8192]{1,0:T(8,128)S(1)}, u32[]{:S(2)}) copy-start(f32[128,8192]{1,0:T(8,128)S(1)} %get-tuple-element.79) | copy-start | bytes 12582916
  1415.5 16.1 copy-start.1
  1431.6 12.2 copy-start.2
  1564.7 728.0 %all-to-all-start.1 = ((f32[8,128,8192]{2,1,0:T(8,128)}), f32[8,128,8192]{2,1,0:T(8,128)}, u32[]{:S(2)}, u32[]{:S(2)}) async-start(f32[8,128,8192]{2,1,0:T(8,128)} %bitcast.166), calls=%async_computation.1 | async-start | bytes 67108864 | tf_op jit(solution)/shard_map/all_to_all | solution.py:18
  1571.8 33.4 %copy-start.4 = (s32[65536]{0:T(1024)S(1)}, s32[65536]{0:T(1024)}, u32[]{:S(2)}) copy-start(s32[65536]{0:T(1024)} %param.6) | copy-start | bytes 786436
  2551.7 26.4 copy-start.5
  2578.1 33.7 %copy-start.6 = (f32[128]{0:T(128)}, f32[128]{0:T(128)S(1)}, u32[]{:S(2)}) copy-start(f32[128]{0:T(128)S(1)} %add_sqrt_fusion) | copy-start | bytes 1540
Sparse Core Ops, SparseCore 0:
  924.0 141.7 all-reduce.2
where the time goes:
time: 2650 us; the launch traced here: 2640 us
  waiting for transfers between devices  829 us (31%)
  blocking collectives  761 us (29%)
  local copies, waits for them, and re-layouts  424 us (16%)
  matrix products  317 us (12%)
  other arithmetic  282 us (11%)
    all_to_all x1, blocking collectives, local(): lax.all_to_all(coeffs, 'band', split_axis=1, concat_axis=0, tiled=True)  735 us
    all_to_all x1, waiting for transfers between devices, local(): lax.all_to_all(ortho_cols, 'band', split_axis=0, concat_axis=1, tiled=True)  687 us
    gather x1, local copies, waits for them, and re-layouts, local(): aligned = jnp.take(ortho, index_map, axis=1)  228 us
    another operation x15, matrix products, local(): lax.linalg.triangular_solve(factor, columns, left_side=True, lower=True)  177 us
    another operation x30, other arithmetic, local(): factor = jnp.linalg.cholesky(margin)  172 us
    psum x1, waiting for transfers between devices, local(): margin = lax.psum(partial_value, ('band', 'coef'))  142 us
    dot_general x1, matrix products, local(): jnp.dot(columns, columns.T, precision=lax.Precision.HIGHEST, preferred_el...  117 us
    unnamed x17, local copies, waits for them, and re-layouts  102 us
  transfers between devices with their start and end apart: 2, of which 2 were waited for; matrix products, arithmetic and copies ran while one was open for 1% of the time, Pallas kernels for 0%

commit v1 on v0

--- a/solution.py
+++ b/solution.py
@@ -12,7 +12,7 @@
     partial_value = jnp.dot(
         columns, columns.T, precision=lax.Precision.HIGHEST, preferred_element_type=jnp.float32
     )
-    margin = lax.psum(partial_value, ("band", "coef"))
+    margin = lax.psum(lax.psum(partial_value, "band"), "coef")
     factor = jnp.linalg.cholesky(margin)
     ortho_cols = lax.linalg.triangular_solve(factor, columns, left_side=True, lower=True)
     ortho = lax.all_to_all(ortho_cols, "band", split_axis=0, concat_axis=1, tiled=True)

time: 2650 us -> 2750 us (1.038)
  waiting for transfers between devices: 829 us -> 931 us
    psum x1 -> x2, waiting for transfers between devices: 142 us -> 242 us  [local(): margin = lax.psum(lax.psum(partial_value, 'band'), 'coef')]
  transfers between devices with their start and end apart: 2 -> 3, of which waited for: 2 -> 3; matrix products, arithmetic and copies ran while one was open for 1% -> 1% of each run, Pallas kernels for 0% -> 0%
where the time goes in v1:
time: 2750 us; the launch traced here: 2740 us
  waiting for transfers between devices  931 us (34%)
  blocking collectives  761 us (28%)
  local copies, waits for them, and re-layouts  424 us (15%)
  matrix products  317 us (12%)
  other arithmetic  282 us (10%)
    all_to_all x1, blocking collectives, local(): lax.all_to_all(coeffs, 'band', split_axis=1, concat_axis=0, tiled=True)  735 us
    all_to_all x1, waiting for transfers between devices, local(): lax.all_to_all(ortho_cols, 'band', split_axis=0, concat_axis=1, tiled=True)  689 us
    psum x2, waiting for transfers between devices, local(): margin = lax.psum(lax.psum(partial_value, 'band'), 'coef')  242 us
    gather x1, local copies, waits for them, and re-layouts, local(): aligned = jnp.take(ortho, index_map, axis=1)  228 us
    another operation x15, matrix products, local(): lax.linalg.triangular_solve(factor, columns, left_side=True, lower=True)  177 us
    another operation x30, other arithmetic, local(): factor = jnp.linalg.cholesky(margin)  172 us
    dot_general x1, matrix products, local(): jnp.dot(columns, columns.T, precision=lax.Precision.HIGHEST, preferred_el...  117 us
    unnamed x17, local copies, waits for them, and re-layouts  102 us
  transfers between devices with their start and end apart: 3, of which 3 were waited for; matrix products, arithmetic and copies ran while one was open for 1% of the time, Pallas kernels for 0%

profile of v1, /device:TPU:0, one launch (start us, length us, event | category | flops | bytes accessed | tf_op | source)
XLA Modules:
  0.0 2741.5 jit_solution(10057939582496905601)
XLA Ops:
  7.2 33.4 %copy.17 = f32[128,65536]{0,1:T(8,128)} copy(f32[128,65536]{1,0:T(8,128)} %param.4) | data formatting | bytes 67108864 | tf_op args[0]
  40.6 31.1 %copy.18 = f32[128,8,8192]{2,0,1:T(8,128)} copy(f32[128,8,8192]{0,2,1:T(8,128)} %bitcast.156) | data formatting | bytes 67108864 | tf_op jit(solution)/shard_map/all_to_all | solution.py:11
  71.7 735.1 %all_to_all.38 = f32[128,8,8192]{2,0,1:T(8,128)} all-to-all(f32[128,8,8192]{2,0,1:T(8,128)} %copy.18), channel_id=1, replica_groups=mesh['band'=8,'coef'=4] {'band'}, dimensions={1} | all-to-all | bytes 67108864 | tf_op jit(solution)/shard_map/all_to_all | solution.py:11
  806.8 117.0 %fusion.74 = f32[1024,1024]{0,1:T(8,128)} fusion(f32[1024,8192]{1,0:T(8,128)} %bitcast.157), kind=kOutput, calls=%fused_computation.177 | convolution fusion | flops 103079215104 | bytes 37748736 | tf_op jit(solution)/shard_map/dot_general | solution.py:12
  923.9 155.6 %all-reduce.4.cloned.1.call-done = f32[1024,1024]{0,1:T(8,128)} async-done(((f32[1024,1024]{0,1:T(8,128)}), f32[1024,1024]{0,1:T(8,128)}) %all-reduce.4.cloned.1.call-update) | async-done | bytes 4194320 | tf_op jit(solution)/shard_map/psum | solution.py:15
  1079.6 86.8 %all-reduce.6.cloned.1.call-done = f32[1024,1024]{0,1:T(8,128)} async-done(((f32[1024,1024]{0,1:T(8,128)}), f32[1024,1024]{0,1:T(8,128)}) %all-reduce.6.cloned.1.call-update) | async-done | bytes 4194320 | tf_op jit(solution)/shard_map/psum | solution.py:15
  1166.4 5.5 copy.20
  1178.4 11.7 cholesky.223
  1190.2 9.8 custom-call.62
  1206.4 11.9 cholesky.244
  1218.9 9.8 custom-call.63
  1232.1 11.7 cholesky.468
  1245.1 9.8 custom-call.64
  1258.4 12.1 cholesky.487
  1271.7 9.8 custom-call.65
  1285.0 11.7 cholesky.506
  1298.0 10.0 custom-call.66
  1311.3 11.7 cholesky.526
  1324.3 9.8 custom-call.67
  1337.1 11.9 cholesky.546
  1350.3 9.8 custom-call.68
  1362.8 11.7 cholesky.564
  1386.2 23.2 while.1
  1409.4 79.0 %custom-call.69 = f32[8,128,128]{1,2,0:T(8,128)S(1)} custom-call(f32[8,128,128]{2,1,0:T(8,128)S(1)} %get-tuple-element.10), custom_call_target="InvertDiagBlocksLowerTriangular" | custom-call | tf_op jit(solution)/shard_map/triangular_solve | solution.py:17
  1488.5 12.6 constant_dynamic-update-slice_fusion.17
  1501.0 6.9 convolution_subtract_fusion.1
  1508.0 8.2 constant_dynamic-update-slice_fusion.16
  1516.2 7.7 convolution_subtract_fusion
  1523.9 8.4 constant_dynamic-update-slice_fusion.15
  1532.3 12.2 fusion.16
  1544.5 13.9 constant_dynamic-update-slice_fusion.14
  1558.4 14.1 fusion.19
  1572.5 12.5 constant_dynamic-update-slice_fusion.13
  1585.0 17.1 convolution_subtract_fusion.2
  1602.1 6.7 constant_dynamic-update-slice_fusion.12
  1608.9 19.3 convolution_subtract_fusion.4
  1628.1 5.8 constant_dynamic-update-slice_fusion.11
  1633.9 23.5 convolution_subtract_fusion.3
  1657.5 7.9 convolution_dynamic-update-slice_fusion
  1665.4 7.1 all-to-all-start.1
  1672.5 33.4 %copy.22 = f32[128,65536]{0,1:T(8,128)} copy(f32[128,65536]{1,0:T(8,128)} %param.5) | data formatting | bytes 67108864 | tf_op args[1]
  1706.1 688.7 %all-to-all-done.1 = f32[8,128,8192]{2,1,0:T(8,128)} async-done(((f32[8,128,8192]{2,1,0:T(8,128)}), f32[8,128,8192]{2,1,0:T(8,128)}, u32[]{:S(2)}, u32[]{:S(2)}) %all-to-all-start.1) | async-done | bytes 33554464 | tf_op jit(solution)/shard_map/all_to_all | solution.py:18
  2394.8 31.0 %copy.21 = f32[128,8,8192]{0,2,1:T(8,128)} copy(f32[128,8,8192]{2,0,1:T(8,128)} %bitcast.35) | data formatting | bytes 67108864 | tf_op jit(solution)/shard_map/all_to_all | solution.py:18
  2425.7 228.0 %gather_fusion = f32[65536,128]{1,0:T(8,128)} fusion(f32[128,65536]{0,1:T(8,128)} %bitcast.154, s32[65536]{0:T(1024)S(1)} %fusion.45), kind=kCustom, calls=%fused_computation | custom fusion | bytes 67371008 | tf_op jit(solution)/shard_map/jit(_take)/gather | solution.py:19
  2653.8 20.7 fusion.1
  2674.5 5.7 psum.30
  2680.3 33.5 %copy.23 = f32[128,65536]{1,0:T(8,128)} copy(f32[128,65536]{0,1:T(8,128)} %bitcast.155) | data formatting | bytes 67108864
  2713.8 20.1 psum.31
  (89 shorter events, 70.0 us)
Async XLA Ops:
  7.2 1072.4 %all-reduce.4.cloned.1.call-start = ((), (), s32[]{:S(2)}) async-start(), calls=%async_computation.2 | async-start | bytes 8388608 | tf_op jit(solution)/shard_map/psum | solution.py:15
  923.8 242.6 %all-reduce.6.cloned.1.call-start = ((), (), s32[]{:S(2)}) async-start(), calls=%async_computation.3 | async-start | bytes 8388608 | tf_op jit(solution)/shard_map/psum | solution.py:15
  1176.4 2.0 copy-start.3
  1501.0 31.3 %copy-start = (f32[128,8192]{1,0:T(8,128)}, f32[128,8192]{1,0:T(8,128)S(1)}, u32[]{:S(2)}) copy-start(f32[128,8192]{1,0:T(8,128)S(1)} %get-tuple-element.79) | copy-start | bytes 12582916
  1516.2 16.1 copy-start.1
  1532.3 12.2 copy-start.2
  1665.4 729.4 %all-to-all-start.1 = ((f32[8,128,8192]{2,1,0:T(8,128)}), f32[8,128,8192]{2,1,0:T(8,128)}, u32[]{:S(2)}, u32[]{:S(2)}) async-start(f32[8,128,8192]{2,1,0:T(8,128)} %bitcast.166), calls=%async_computation.1 | async-start | bytes 67108864 | tf_op jit(solution)/shard_map/all_to_all | solution.py:18
  1672.5 33.4 %copy-start.4 = (s32[65536]{0:T(1024)S(1)}, s32[65536]{0:T(1024)}, u32[]{:S(2)}) copy-start(s32[65536]{0:T(1024)} %param.6) | copy-start | bytes 786436
  2653.8 26.4 copy-start.5
  2680.1 33.7 %copy-start.6 = (f32[128]{0:T(128)}, f32[128]{0:T(128)S(1)}, u32[]{:S(2)}) copy-start(f32[128]{0:T(128)S(1)} %add_sqrt_fusion) | copy-start | bytes 1540
Sparse Core Ops, SparseCore 0:
  924.0 155.5 all-reduce.3
  1081.9 84.4 all-reduce.5
